TPU v7x, 256 devices: a whole 4x4x8 slice. The times are simulated.
256 devices in a mesh: dp: 16 (over x, y_hi, core), fsdp: 16 (over y_lo, z).
Axes of the slice: x: 4, y: 4 (y_hi: 2, y_lo: 2; y = y_hi * 2 + y_lo), z: 8, core: 2. Of those that a mesh axis runs over, the one named last changes fastest.
Arguments:
- tokens: bfloat16 [8192, 2048], P('dp'), may hold values from -6 to 6
- expert_ids: int32 [8192, 2], P('dp'), may hold values from 0 to 7, as said below
- route_probs: float32 [8192, 2], P('dp'), may hold values from 0.1 to 1
- gate_w: bfloat16 [2, 2048, 7168], P(None, 'dp', 'fsdp'), may hold values from -0.125 to 0.125
- up_w: bfloat16 [2, 2048, 7168], P(None, 'dp', 'fsdp'), may hold values from -0.125 to 0.125
- down_w: bfloat16 [2, 7168, 2048], P(None, 'fsdp', 'dp'), may hold values from -0.0625 to 0.0625
- out_grad: bfloat16 [8192, 2048], P('dp'), may hold values from -6 to 6
Outputs:
- mixed: bfloat16 [8192, 2048], P('dp')
- token_grad: bfloat16 [8192, 2048], P('dp')
- gate_grad: bfloat16 [2, 2048, 7168], P(None, 'dp', 'fsdp')
- up_grad: bfloat16 [2, 2048, 7168], P(None, 'dp', 'fsdp')
- down_grad: bfloat16 [2, 7168, 2048], P(None, 'fsdp', 'dp')
Inputs may be any that keep to these rules, and one draw needn't show every extreme that they name: `expert_ids`: the two entries of a row differ. In each aligned block of 512 rows (the rows of one index of dp) every expert is named by at most 256 rows, and one of experts 0 to 1 by exactly 256 rows.
All inputs are finite; a program needn't handle non-finite values.
Results may differ from a plain program's by a relative error of at most 0.018.
Values may be sent and summed in bfloat16 or wider, within the bound.
A program may use at most 128 MiB of HBM per device.

v0:
```python
import jax
import jax.numpy as jnp
from jax import lax
from jax.sharding import PartitionSpec as P


def slot_layout(expert_ids, route_probs, expert, slot_cap):
    token_count = expert_ids.shape[0]
    matches = expert_ids == expert
    chosen = jnp.any(matches, axis=1)
    weight_token = jnp.sum(jnp.where(matches, route_probs, jnp.float32(0.0)), axis=1)
    position = jnp.cumsum(chosen.astype(jnp.int32)) - 1
    slot_index = lax.broadcasted_iota(jnp.int32, (slot_cap, token_count), 0)
    token_index = lax.broadcasted_iota(jnp.int32, (slot_cap, token_count), 1)
    matched_slots = (position[None, :] == slot_index) & chosen[None, :]
    slot_token = jnp.sum(jnp.where(matched_slots, token_index, 0), axis=1)
    slot_valid = jnp.any(matched_slots, axis=1)
    slot_weight = jnp.where(slot_valid, jnp.take(weight_token, slot_token), jnp.float32(0.0))
    token_slot = jnp.clip(position, 0, slot_cap - 1)
    return (chosen, token_slot, slot_token, slot_valid, slot_weight)


def group_total(partial_value):
    return lax.psum(partial_value.astype(jnp.bfloat16), "fsdp")


def body(tokens, expert_ids, route_probs, gate_w, up_w, down_w, out_grad):
    token_count = tokens.shape[0]
    width = tokens.shape[1]
    slot_cap = token_count // 2
    window = gate_w.shape[0]
    mixed_part = jnp.zeros((token_count, width), jnp.float32)
    stored = []
    for expert in range(window):
        chosen, token_slot, slot_token, slot_valid, slot_weight = slot_layout(
            expert_ids, route_probs, expert, slot_cap
        )
        gate_full, up_full, down_full = (
            lax.all_gather(gate_w[expert], "dp", axis=0, tiled=True),
            lax.all_gather(up_w[expert], "dp", axis=0, tiled=True),
            lax.all_gather(down_w[expert], "dp", axis=1, tiled=True),
        )
        slot_input = jnp.take(tokens, slot_token, axis=0) * slot_valid[:, None].astype(tokens.dtype)
        gate_act = jnp.dot(slot_input, gate_full, preferred_element_type=jnp.float32)
        up_act = jnp.dot(slot_input, up_full, preferred_element_type=jnp.float32)
        hidden = (jax.nn.silu(gate_act) * up_act).astype(jnp.bfloat16)
        expert_out = (
            jnp.dot(hidden, down_full, preferred_element_type=jnp.float32) * slot_weight[:, None]
        )
        mixed_part = mixed_part + jnp.where(
            chosen[:, None], jnp.take(expert_out, token_slot, axis=0), jnp.float32(0.0)
        )
        stored.append(
            (
                chosen,
                token_slot,
                slot_token,
                slot_weight,
                slot_input,
                gate_act,
                up_act,
                hidden,
                gate_full,
                up_full,
                down_full,
            )
        )
    mixed = group_total(mixed_part)
    grad_part = jnp.zeros((token_count, width), jnp.float32)
    gate_grads, up_grads, down_grads = ([], [], [])
    for expert in range(window):
        (
            chosen,
            token_slot,
            slot_token,
            slot_weight,
            slot_input,
            gate_act,
            up_act,
            hidden,
            gate_full,
            up_full,
            down_full,
        ) = stored[expert]
        slot_grad = (
            jnp.take(out_grad, slot_token, axis=0).astype(jnp.float32) * slot_weight[:, None]
        ).astype(jnp.bfloat16)
        down_term = lax.dot_general(
            hidden, slot_grad, (((0,), (0,)), ((), ())), preferred_element_type=jnp.float32
        )
        hidden_grad = lax.dot_general(
            slot_grad, down_full, (((1,), (1,)), ((), ())), preferred_element_type=jnp.float32
        )
        sigma = jax.nn.sigmoid(gate_act)
        up_act_grad = (hidden_grad * gate_act * sigma).astype(jnp.bfloat16)
        gate_act_grad = (hidden_grad * up_act * sigma * (1.0 + gate_act * (1.0 - sigma))).astype(
            jnp.bfloat16
        )
        gate_term = lax.dot_general(
            slot_input, gate_act_grad, (((0,), (0,)), ((), ())), preferred_element_type=jnp.float32
        )
        up_term = lax.dot_general(
            slot_input, up_act_grad, (((0,), (0,)), ((), ())), preferred_element_type=jnp.float32
        )
        input_grad = lax.dot_general(
            gate_act_grad, gate_full, (((1,), (1,)), ((), ())), preferred_element_type=jnp.float32
        )
        input_grad = input_grad + lax.dot_general(
            up_act_grad, up_full, (((1,), (1,)), ((), ())), preferred_element_type=jnp.float32
        )
        grad_part = grad_part + jnp.where(
            chosen[:, None], jnp.take(input_grad, token_slot, axis=0), jnp.float32(0.0)
        )
        gate_sum, up_sum, down_sum = (
            lax.psum_scatter(
                gate_term.astype(jnp.bfloat16), "dp", scatter_dimension=0, tiled=True
            ).astype(jnp.float32),
            lax.psum_scatter(
                up_term.astype(jnp.bfloat16), "dp", scatter_dimension=0, tiled=True
            ).astype(jnp.float32),
            lax.psum_scatter(
                down_term.astype(jnp.bfloat16), "dp", scatter_dimension=1, tiled=True
            ).astype(jnp.float32),
        )
        gate_grads.append(gate_sum.astype(jnp.bfloat16))
        up_grads.append(up_sum.astype(jnp.bfloat16))
        down_grads.append(down_sum.astype(jnp.bfloat16))
    gate_grad = jnp.stack(gate_grads)
    up_grad = jnp.stack(up_grads)
    down_grad = jnp.stack(down_grads)
    token_grad = group_total(grad_part)
    return (mixed, token_grad, gate_grad, up_grad, down_grad)


def solution(mesh):
    placed = (
        P("dp", None),
        P("dp", None),
        P("dp", None),
        P(None, "dp", "fsdp"),
        P(None, "dp", "fsdp"),
        P(None, "fsdp", "dp"),
        P("dp", None),
    )
    return jax.shard_map(
        body,
        mesh=mesh,
        in_specs=placed,
        out_specs=(
            P("dp", None),
            P("dp", None),
            P(None, "dp", "fsdp"),
            P(None, "dp", "fsdp"),
            P(None, "fsdp", "dp"),
        ),
        check_vma=False,
    )
```

profile of v0, /device:TPU:8, one launch (start us, length us, event | category | flops | bytes accessed | tf_op | source)
XLA Modules:
  0.0 1002.2 jit_solution(5504983384310768062)
XLA Ops:
  19.5 5.2 gather_fusion.8
  24.7 42.1 %all-gather.21.cloned.1.call-done = bf16[1,2048,448]{1,2,0:T(8,128)(2,1)} async-done(((bf16[1,128,448]{1,2,0:T(8,128)(2,1)}), bf16[1,2048,448]{1,2,0:T(8,128)(2,1)}) %all-gather.21.cloned.1.call-update) | async-done | bytes 1835024 | tf_op jit(solution)/shard_map/all_gather | solution.py:40
  69.9 52.5 %all-gather.19.cloned.1.call-done = bf16[1,2048,448]{1,2,0:T(8,128)(2,1)} async-done(((bf16[1,128,448]{1,2,0:T(8,128)(2,1)}), bf16[1,2048,448]{1,2,0:T(8,128)(2,1)}) %all-gather.19.cloned.1.call-update) | async-done | bytes 1835024 | tf_op jit(solution)/shard_map/all_gather | solution.py:39
  125.4 52.0 %all-gather.23.cloned.1.call-done = bf16[1,448,2048]{2,1,0:T(8,128)(2,1)} async-done(((bf16[1,448,128]{2,1,0:T(8,128)(2,1)}), bf16[1,448,2048]{2,1,0:T(8,128)(2,1)}) %all-gather.23.cloned.1.call-update) | async-done | bytes 1835024 | tf_op jit(solution)/shard_map/all_gather | solution.py:41
  177.4 3.7 multiply_convert_fusion.2
  183.8 3.8 copy.22
  190.2 4.3 gather_fusion.6
  196.7 36.2 %all-gather.15.cloned.1.call-done = bf16[1,2048,448]{1,2,0:T(8,128)(2,1)} async-done(((bf16[1,128,448]{1,2,0:T(8,128)(2,1)}), bf16[1,2048,448]{1,2,0:T(8,128)(2,1)}) %all-gather.15.cloned.1.call-update) | async-done | bytes 1835024 | tf_op jit(solution)/shard_map/all_gather | solution.py:40
  236.0 52.4 %all-gather.13.cloned.1.call-done = bf16[1,2048,448]{1,2,0:T(8,128)(2,1)} async-done(((bf16[1,128,448]{1,2,0:T(8,128)(2,1)}), bf16[1,2048,448]{1,2,0:T(8,128)(2,1)}) %all-gather.13.cloned.1.call-update) | async-done | bytes 1835024 | tf_op jit(solution)/shard_map/all_gather | solution.py:39
  291.4 51.8 %all-gather.17.cloned.1.call-done = bf16[1,448,2048]{2,1,0:T(8,128)(2,1)} async-done(((bf16[1,448,128]{2,1,0:T(8,128)(2,1)}), bf16[1,448,2048]{2,1,0:T(8,128)(2,1)}) %all-gather.17.cloned.1.call-update) | async-done | bytes 1835024 | tf_op jit(solution)/shard_map/all_gather | solution.py:41
  343.2 3.3 multiply_convert_fusion.4
  370.1 3.6 gather_fusion.2
  376.8 3.6 gather_fusion.7
  382.7 3.6 gather_fusion.5
  389.4 3.6 gather_fusion.9
  393.0 9.4 fusion.1
  402.4 22.7 %reduce-scatter.29.cloned.1.call-done = bf16[128,448]{1,0:T(8,128)(2,1)} async-done(((bf16[2048,448]{1,0:T(8,128)(2,1)}), bf16[128,448]{1,0:T(8,128)(2,1)}) %reduce-scatter.29.cloned.1.call-update) | async-done | bytes 114704
  426.1 80.9 %reduce-scatter.27.cloned.1.call-done = bf16[128,448]{1,0:T(8,128)(2,1)} async-done(((bf16[2048,448]{1,0:T(8,128)(2,1)}), bf16[128,448]{1,0:T(8,128)(2,1)}) %reduce-scatter.27.cloned.1.call-update) | async-done | bytes 114704
  508.1 80.9 %reduce-scatter.23.cloned.1.call-done = bf16[128,448]{1,0:T(8,128)(2,1)} async-done(((bf16[2048,448]{1,0:T(8,128)(2,1)}), bf16[128,448]{1,0:T(8,128)(2,1)}) %reduce-scatter.23.cloned.1.call-update) | async-done | bytes 114704
  590.1 80.8 %reduce-scatter.19.cloned.1.call-done = bf16[128,448]{1,0:T(8,128)(2,1)} async-done(((bf16[2048,448]{1,0:T(8,128)(2,1)}), bf16[128,448]{1,0:T(8,128)(2,1)}) %reduce-scatter.19.cloned.1.call-update) | async-done | bytes 114704
  671.9 81.0 %reduce-scatter.25.cloned.1.call-done = bf16[128,448]{1,0:T(8,128)(2,1)} async-done(((bf16[2048,448]{1,0:T(8,128)(2,1)}), bf16[128,448]{1,0:T(8,128)(2,1)}) %reduce-scatter.25.cloned.1.call-update) | async-done | bytes 114704
  753.9 80.8 %reduce-scatter.21.cloned.1.call-done = bf16[128,448]{1,0:T(8,128)(2,1)} async-done(((bf16[2048,448]{1,0:T(8,128)(2,1)}), bf16[128,448]{1,0:T(8,128)(2,1)}) %reduce-scatter.21.cloned.1.call-update) | async-done | bytes 114704
  837.9 153.1 %all-reduce.3.cloned.1.call-done = (bf16[512,2048]{1,0:T(8,128)(2,1)}, bf16[512,2048]{1,0:T(8,128)(2,1)}) async-done(((bf16[512,2048]{1,0:T(8,128)(2,1)}, bf16[512,2048]{1,0:T(8,128)(2,1)}), (bf16[512,2048]{1,0:T(8,128)(2,1)}, bf16[512,2048]{1,0:T(8,128)(2,1)})) %all-reduce.3.cloned.1.call-update) | async-done | bytes 4194320 | tf_op jit(solution)/shard_map/psum | solution.py:24
  991.0 3.3 copy.26
  (133 shorter events, 73.2 us)
Async XLA Ops:
  7.2 10.9 %copy-start = (bf16[512,2048]{1,0:T(8,128)(2,1)S(1)}, bf16[512,2048]{1,0:T(8,128)(2,1)}, u32[]{:S(2)}) copy-start(bf16[512,2048]{1,0:T(8,128)(2,1)} %param.13) | copy-start | bytes 6291460
  7.2 7.1 copy-start.18
  7.2 8.9 copy-start.19
  7.2 59.6 %all-gather.21.cloned.1.call-start = ((), (), s32[]{:S(2)}) async-start(), calls=%async_computation.10 | async-start | bytes 1949696 | tf_op jit(solution)/shard_map/all_gather | solution.py:40
  9.1 113.3 %all-gather.19.cloned.1.call-start = ((), (), s32[]{:S(2)}) async-start(), calls=%async_computation.9 | async-start | bytes 1949696 | tf_op jit(solution)/shard_map/all_gather | solution.py:39
  10.8 166.6 %all-gather.23.cloned.1.call-start = ((), (), s32[]{:S(2)}) async-start(), calls=%async_computation.11 | async-start | bytes 1949696 | tf_op jit(solution)/shard_map/all_gather | solution.py:41
  12.5 220.4 %all-gather.15.cloned.1.call-start = ((), (), s32[]{:S(2)}) async-start(), calls=%async_computation.7 | async-start | bytes 1949696 | tf_op jit(solution)/shard_map/all_gather | solution.py:40
  13.1 275.2 %all-gather.13.cloned.1.call-start = ((), (), s32[]{:S(2)}) async-start(), calls=%async_computation.6 | async-start | bytes 1949696 | tf_op jit(solution)/shard_map/all_gather | solution.py:39
  13.7 329.5 %all-gather.17.cloned.1.call-start = ((), (), s32[]{:S(2)}) async-start(), calls=%async_computation.8 | async-start | bytes 1949696 | tf_op jit(solution)/shard_map/all_gather | solution.py:41
  14.3 410.8 %reduce-scatter.29.cloned.1.call-start = ((), (), s32[]{:S(2)}) async-start(), calls=%async_computation.17 | async-start | bytes 2228224
  177.4 4.3 copy-start.7
  187.6 319.5 %reduce-scatter.27.cloned.1.call-start = ((), (), s32[]{:S(2)}) async-start(), calls=%async_computation.16 | async-start | bytes 2228224
  190.2 42.7 %copy-start.5 = (bf16[256,2048]{1,0:T(8,128)(2,1)S(1)}, bf16[256,2048]{1,0:T(8,128)(2,1)}, u32[]{:S(2)}) copy-start(bf16[256,2048]{1,0:T(8,128)(2,1)} %gather_fusion) | copy-start | bytes 3145732
  194.5 148.7 %copy-start.6 = (bf16[256,2048]{1,0:T(8,128)(2,1)}, bf16[256,2048]{1,0:T(8,128)(2,1)S(1)}, u32[]{:S(2)}) copy-start(bf16[256,2048]{1,0:T(8,128)(2,1)S(1)} %gather_fusion.6) | copy-start | bytes 3145732
  351.8 237.3 %reduce-scatter.23.cloned.1.call-start = ((), (), s32[]{:S(2)}) async-start(), calls=%async_computation.14 | async-start | bytes 2228224
  356.3 314.5 %reduce-scatter.19.cloned.1.call-start = ((), (), s32[]{:S(2)}) async-start(), calls=%async_computation.12 | async-start | bytes 2228224
  360.8 392.0 %reduce-scatter.25.cloned.1.call-start = ((), (), s32[]{:S(2)}) async-start(), calls=%async_computation.15 | async-start | bytes 2228224
  364.2 470.5 %reduce-scatter.21.cloned.1.call-start = ((), (), s32[]{:S(2)}) async-start(), calls=%async_computation.13 | async-start | bytes 2228224
  367.5 623.5 %all-reduce.3.cloned.1.call-start = ((), (), s32[]{:S(2)}) async-start(), calls=%async_computation.18 | async-start | bytes 8388608 | tf_op jit(solution)/shard_map/psum | solution.py:24
  370.1 3.6 copy-start.15
  376.8 3.6 copy-start.11
  382.7 3.6 copy-start.9
  991.0 3.3 copy-start.2
  991.0 4.6 copy-start.1
  (9 other events, 19.0 us)
Sparse Core Ops, SparseCore 0:
  11.2 55.5 all-gather.20
  69.9 52.4 all-gather.18
  125.0 52.4 all-gather.22
  180.4 52.4 all-gather.14
  235.9 52.4 all-gather.12
  290.8 52.4 all-gather.16
  347.5 77.5 reduce-scatter.28
  429.3 77.7 reduce-scatter.26
  511.3 77.6 reduce-scatter.22
  593.1 77.7 reduce-scatter.18
  675.1 77.7 reduce-scatter.24
  756.9 77.7 reduce-scatter.20
  838.0 152.9 all-reduce.2
where the time goes:
time: 1000 us
  waiting for transfers between devices  869 us (87%)
  local copies, waits for them, and re-layouts  65.4 us (7%)
  matrix products  39.4 us (4%)
  between operations  14.3 us (1%)
  other arithmetic  13.1 us (1%)
    unnamed x19, waiting for transfers between devices  429 us
    psum x1, waiting for transfers between devices, group_total(): return lax.psum(partial_value.astype(jnp.bfloat16), 'fsdp')  153 us
    all_gather x2, waiting for transfers between devices, body(): lax.all_gather(gate_w[expert], 'dp', axis=0, tiled=True)  105 us
    all_gather x2, waiting for transfers between devices, body(): lax.all_gather(down_w[expert], 'dp', axis=1, tiled=True)  104 us
    all_gather x2, waiting for transfers between devices, body(): lax.all_gather(up_w[expert], 'dp', axis=0, tiled=True)  78.4 us
    unnamed x54, local copies, waits for them, and re-layouts  28.4 us
  transfers between devices with their start and end apart: 13, of which 13 were waited for; matrix products, arithmetic and copies ran while one was open for 11% of the time, Pallas kernels for 0%

commit v1 on v0

v1 whole, which is shorter than its diff:
```python
import heapq

import jax
import jax.numpy as jnp
from jax import lax
from jax.experimental import pallas as pl
from jax.experimental.pallas import tpu as pltpu
from jax.sharding import PartitionSpec as P

MESH = pl.DeviceIdType.MESH
BF = jnp.bfloat16
F32 = jnp.float32
NX, NZ = 4, 8
LANE = 128
NSEM = 256

NT = (((1,), (1,)), ((), ()))
NN = (((1,), (0,)), ((), ()))
TN = (((0,), (0,)), ((), ()))


def dot(a, b, dims):
    return lax.dot_general(a, b, dims, preferred_element_type=F32)


class Clock:
    def __init__(self):
        self.heap, self.now, self.count = [], 0.0, 0

    def spawn(self, stream, delay=0.0):
        self.count += 1
        heapq.heappush(self.heap, (self.now + delay, self.count, stream))

    def busy(self, us):
        self.now += us

    def run(self):
        while self.heap:
            at, _, stream = heapq.heappop(self.heap)
            self.now = max(self.now, at)
            try:
                delay = next(stream)
            except StopIteration:
                continue
            self.spawn(stream, delay)


def add_into(out, terms, rows=64):
    lead = out.shape[:-2]
    total = 1
    for n in lead:
        total *= n
    height = out.shape[-2]
    while height % rows:
        rows //= 2
    steps = height // rows

    def step(i, carry):
        at, rest = lax.rem(i, steps), lax.div(i, steps)
        index = []
        for n in reversed(lead):
            index.append(lax.rem(rest, n))
            rest = lax.div(rest, n)
        index = tuple(reversed(index)) + (pl.ds(pl.multiple_of(at * rows, rows), rows), slice(None))
        value = terms[0][index].astype(F32)
        for term in terms[1:]:
            value = value + term[index].astype(F32)
        out[index] = value.astype(out.dtype)
        return carry

    lax.fori_loop(0, total * steps, step, 0)


def kernel(
    w_in, tok_ref, grad_ref, ids_ref, probs_ref,
    mixed_ref, tgrad_ref, wgrad_ref,
    w_all, dw, cr, xa, xb, ys, yr,
    a0, a1, z0, z1, y0s, y0r, y1r, s0, s1,
    pick, xin, gin, gt, ut, ht, gat, uat,
    send_sem, recv_sem, local_sem,
):
    dp, fs = lax.axis_index("dp"), lax.axis_index("fsdp")
    x, yh, c = dp // 4, (dp // 2) % 2, dp % 2
    yl, z = fs // NZ, fs % NZ
    experts, mats, hid, _ = w_in.shape
    tok, width = tok_ref.shape
    slots = tok // 2
    half = hid // 2
    core = (x * 4 + yh * 2 + 1 - c, fs)
    yhp = (x * 4 + (1 - yh) * 2 + c, fs)
    xr = (((x + 1) % NX) * 4 + yh * 2 + c, fs)
    xl = (((x + 3) % NX) * 4 + yh * 2 + c, fs)
    ylp = (dp, (1 - yl) * NZ + z)
    zr = (dp, yl * NZ + (z + 1) % NZ)
    zl = (dp, yl * NZ + (z + 7) % NZ)

    sent = []

    def send(src, dst, device):
        i = len(sent)
        copy = pltpu.make_async_remote_copy(
            src_ref=src, dst_ref=dst, send_sem=send_sem.at[i], recv_sem=recv_sem.at[i],
            device_id=device, device_id_type=MESH,
        )
        copy.start()
        sent.append(copy)
        return copy

    barrier = pltpu.get_barrier_semaphore()
    for peer in (core, yhp, xr, xl, ylp, zr, zl):
        pl.semaphore_signal(barrier, inc=1, device_id=peer, device_id_type=MESH)
    pl.semaphore_wait(barrier, 7)

    clock = Clock()

    from_core = [[] for _ in range(experts)]
    own_block = []

    def cols(block):
        return pl.ds(pl.multiple_of(block * LANE, LANE), LANE)

    def w_block(e, block, rows=slice(None)):
        return w_all.at[e, :, rows, cols(block)]

    def to_core(e, src, block, rows=slice(None)):
        from_core[e].append(send(src, w_block(e, block, rows), core))

    def gather_row(e, row, src):
        me = x * 4 + row * 2 + c
        left = ((x + 3) % NX) * 4 + row * 2 + c
        right = ((x + 1) % NX) * 4 + row * 2 + c
        far = ((x + 2) % NX) * 4 + row * 2 + c
        top, low = pl.ds(0, half), pl.ds(half, half)
        go_r = send(src, w_block(e, me), xr)
        go_l = send(src, w_block(e, me), xl)
        to_core(e, src, me)
        yield 9.0
        go_r.wait_recv()
        on_r = send(w_block(e, left, top), w_block(e, left, top), xr)
        to_core(e, w_block(e, left), left)
        yield 0.0
        go_l.wait_recv()
        on_l = send(w_block(e, right, low), w_block(e, right, low), xl)
        to_core(e, w_block(e, right), right)
        yield 6.0
        on_r.wait_recv()
        to_core(e, w_block(e, far, top), far, top)
        yield 0.0
        on_l.wait_recv()
        to_core(e, w_block(e, far, low), far, low)

    def gather_other(e, wait):
        copy = send(w_in.at[e], w_block(e, dp), yhp)
        yield wait
        copy.wait_recv()
        block = x * 4 + (1 - yh) * 2 + c
        yield from gather_row(e, 1 - yh, w_block(e, block))

    def scatter_grads(e):
        copies = {}
        for k in (2, 1, 3, 0):
            copies[k] = send(dw.at[e, 1 - c, (x + k) % NX], cr.at[e, k], core)
        yield 2.0

        def piece(k):
            return dw.at[e, c, (x + k) % NX]

        copies[2].wait_recv()
        add_into(piece(2), [piece(2), cr.at[e, 2]])
        top, low = pl.ds(0, half), pl.ds(half, half)
        far = (x + 2) % NX
        go_r = send(dw.at[e, c, far, :, :, top], xa.at[e, 0], xr)
        go_l = send(dw.at[e, c, far, :, :, low], xa.at[e, 1], xl)
        yield 1.0
        copies[1].wait_recv()
        add_into(piece(1), [piece(1), cr.at[e, 1]])
        yield 1.0
        copies[3].wait_recv()
        add_into(piece(3), [piece(3), cr.at[e, 3]])
        yield 6.0
        go_r.wait_recv()
        at = dw.at[e, c, (x + 1) % NX, :, :, top]
        add_into(at, [at, xa.at[e, 0]], 32)
        on_r = send(piece(1), xb.at[e, 0], xr)
        yield 0.0
        go_l.wait_recv()
        at = dw.at[e, c, (x + 3) % NX, :, :, low]
        add_into(at, [at, xa.at[e, 1]], 32)
        on_l = send(piece(3), xb.at[e, 1], xl)
        yield 1.0
        copies[0].wait_recv()
        yield 14.0
        on_r.wait_recv()
        on_l.wait_recv()
        other = 1 - yh
        add_into(ys.at[e], [piece(0).at[other], cr.at[e, 0, other], xb.at[e, 0, other], xb.at[e, 1, other]])
        last = send(ys.at[e], yr.at[e], yhp)
        yield 12.0
        last.wait_recv()
        add_into(
            wgrad_ref.at[e],
            [piece(0).at[yh], cr.at[e, 0, yh], xb.at[e, 0, yh], xb.at[e, 1, yh], yr.at[e]],
        )

    summed = [0, 0]

    def sum_outputs(e):
        def piece(k):
            return a0.at[e, (z + k) % NZ]

        h = NZ // 2
        go_r = send(piece(h).at[0], z0.at[e, 0, 0, 0], zr)
        go_l = send(piece(h).at[1], z0.at[e, 1, 0, 1], zl)
        for k in range(1, h):
            yield 3.0 if k == 1 else 5.0
            go_r.wait_recv()
            if k == 1:
                add_into(piece(h - k).at[0], [piece(h - k).at[0], z0.at[e, 0, 0, 0]])
            else:
                add_into(piece(h - k), [piece(h - k), z0.at[e, 0, k - 1]])
            go_r = send(piece(h - k), z0.at[e, 0, k], zr)
            go_l.wait_recv()
            if k == 1:
                add_into(piece(h + k).at[1], [piece(h + k).at[1], z0.at[e, 1, 0, 1]])
            else:
                add_into(piece(h + k), [piece(h + k), z0.at[e, 1, k - 1]])
            go_l = send(piece(h + k), z0.at[e, 1, k], zl)
        yield 5.0
        go_r.wait_recv()
        go_l.wait_recv()
        other = 1 - yl
        add_into(y0s.at[e], [piece(0).at[other], z0.at[e, 0, h - 1, other], z0.at[e, 1, h - 1, other]])
        last = send(y0s.at[e], y0r.at[e], ylp)
        yield 3.0
        last.wait_recv()
        add_into(s0.at[e], [piece(0).at[yl], z0.at[e, 0, h - 1, yl], z0.at[e, 1, h - 1, yl], y0r.at[e]])
        summed[0] += 1

    def sum_grads(e):
        def piece(k):
            return a1.at[e, yl, (z + k) % NZ]

        h = NZ // 2
        order = [h] + [k for i in range(1, h) for k in (h - i, h + i)] + [0]
        first = {}
        for k in order:
            first[k] = send(a1.at[e, 1 - yl, (z + k) % NZ], y1r.at[e, k], ylp)

        def take(k):
            first[k].wait_recv()
            add_into(piece(k), [piece(k), y1r.at[e, k]])

        yield 3.0
        take(h)
        hs = slots // 2
        top, low = pl.ds(0, hs), pl.ds(hs, hs)
        far = (z + h) % NZ
        go_r = send(a1.at[e, yl, far, top], z1.at[e, 0, 0, top], zr)
        go_l = send(a1.at[e, yl, far, low], z1.at[e, 1, 0, low], zl)
        for k in range(1, h):
            yield 3.0
            take(h - k)
            take(h + k)
            go_r.wait_recv()
            if k == 1:
                at = a1.at[e, yl, (z + h - k) % NZ, top]
                add_into(at, [at, z1.at[e, 0, 0, top]])
            else:
                add_into(piece(h - k), [piece(h - k), z1.at[e, 0, k - 1]])
            go_r = send(piece(h - k), z1.at[e, 0, k], zr)
            go_l.wait_recv()
            if k == 1:
                at = a1.at[e, yl, (z + h + k) % NZ, low]
                add_into(at, [at, z1.at[e, 1, 0, low]])
            else:
                add_into(piece(h + k), [piece(h + k), z1.at[e, 1, k - 1]])
            go_l = send(piece(h + k), z1.at[e, 1, k], zl)
        yield 3.0
        first[0].wait_recv()
        go_r.wait_recv()
        go_l.wait_recv()
        add_into(s1.at[e], [piece(0), y1r.at[e, 0], z1.at[e, 0, h - 1], z1.at[e, 1, h - 1]])
        summed[1] += 1

    def place(out, sums):
        value = dot(pick[0], sums[0], TN)
        for e in range(1, experts):
            value = value + dot(pick[e], sums[e], TN)
        out[:, cols(fs)] = value.astype(out.dtype)

    def share_outputs():
        while summed[0] < experts:
            yield 1.0
        place(mixed_ref, s0)

        def at(y, k):
            return mixed_ref.at[:, cols(y * NZ + (z + k) % NZ)]

        copy = send(at(yl, 0), at(yl, 0), ylp)
        yield 3.0
        copy.wait_recv()
        h = NZ // 2
        go_r = [send(at(y, 0), at(y, 0), zr) for y in range(2)]
        go_l = [send(at(y, 0), at(y, 0), zl) for y in range(2)]
        for k in range(1, h):
            yield 5.0
            for y in range(2):
                go_r[y].wait_recv()
                go_r[y] = send(at(y, -k + NZ), at(y, -k + NZ), zr) if k < h - 1 or y == 0 else None
                go_l[y].wait_recv()
                go_l[y] = send(at(y, k), at(y, k), zl) if k < h - 1 or y == 1 else None
        yield 4.0
        go_r[0].wait_recv()
        go_l[1].wait_recv()

    def share_grads():
        while summed[1] < experts:
            yield 1.0
        place(tgrad_ref, s1)
        ht_ = tok // 2
        top, low = pl.ds(0, ht_), pl.ds(ht_, ht_)

        def at(k, rows=slice(None)):
            return tgrad_ref.at[rows, cols(yl * NZ + (z + k) % NZ)]

        across = []

        def cross(k, rows=slice(None)):
            across.append(send(at(k, rows), at(k, rows), ylp))

        h = NZ // 2
        go_r, go_l = send(at(0), at(0), zr), send(at(0), at(0), zl)
        cross(0)
        for k in range(1, h):
            yield 3.0
            rows_r, rows_l = (slice(None), slice(None)) if k < h - 1 else (top, low)
            go_r.wait_recv()
            go_r = send(at(NZ - k, rows_r), at(NZ - k, rows_r), zr)
            cross(NZ - k)
            go_l.wait_recv()
            go_l = send(at(k, rows_l), at(k, rows_l), zl)
            cross(k)
        yield 3.0
        go_r.wait_recv()
        cross(h, top)
        go_l.wait_recv()
        cross(h, low)
        yield 4.0
        for copy in across:
            copy.wait_recv()

    def slot_rows(e):
        hit = ids_ref[...] == e
        chosen = jnp.max(hit.astype(F32), axis=0, keepdims=True)
        weight = jnp.sum(jnp.where(hit, probs_ref[...], 0.0), axis=0, keepdims=True)
        before = lax.broadcasted_iota(jnp.int32, (tok, tok), 0)
        after = lax.broadcasted_iota(jnp.int32, (tok, tok), 1)
        upper = (before <= after).astype(F32).astype(BF)
        count = dot(jnp.broadcast_to(chosen, (16, tok)).astype(BF), upper, NN)[0:1, :]
        place_of = jnp.where(chosen > 0.0, count - 1.0, -1.0).astype(jnp.int32)
        rows = lax.broadcasted_iota(jnp.int32, (slots, tok), 0)
        mine = (jnp.broadcast_to(place_of, (slots, tok)) == rows).astype(F32)
        slot_weight = jnp.sum(mine * weight, axis=1, keepdims=True)
        pick[e] = mine.astype(BF)
        return slot_weight

    part = 512

    def compute():
        weights = []
        for e in range(experts):
            weights.append(slot_rows(e))
            for j in range(0, width, part):
                at = pl.ds(j, part)
                xin[e, :, at] = dot(pick[e], tok_ref[:, at], NN).astype(BF)
                gin[e, :, at] = (dot(pick[e], grad_ref[:, at], NN) * weights[e]).astype(BF)
            clock.busy(3.0)
            yield 0.0
        for e in range(experts):
            while len(from_core[e]) < 10:
                yield 1.0
            yield 2.0
            own_block[e].wait()
            for copy in from_core[e]:
                copy.wait_recv()
            gt[...] = dot(w_all[e, 0], xin[e], NT)
            ut[...] = dot(w_all[e, 1], xin[e], NT)
            clock.busy(1.5)
            yield 0.0
            gate = gt[...]
            sig = 1.0 / (1.0 + jnp.exp(-gate))
            ht[...] = (gate * sig * ut[...]).astype(BF)
            for j in range(0, width, part):
                value = dot(ht[...], w_all[e, 2, :, pl.ds(j, part)], TN) * weights[e]
                for b in range(part // LANE):
                    f = j // LANE + b
                    a0[e, f % NZ, f // NZ] = value[:, b * LANE : (b + 1) * LANE].astype(BF)
            clock.busy(1.5)
            clock.spawn(sum_outputs(e))
            yield 0.0
            back = dot(w_all[e, 2], gin[e], NT)
            gate = gt[...]
            sig = 1.0 / (1.0 + jnp.exp(-gate))
            uat[...] = (back * gate * sig).astype(BF)
            gat[...] = (back * ut[...] * sig * (1.0 + gate * (1.0 - sig))).astype(BF)
            clock.busy(1.5)
            yield 0.0
            for j in range(0, width, part):
                at = pl.ds(j, part)
                value = dot(gat[...], w_all[e, 0, :, at], TN) + dot(uat[...], w_all[e, 1, :, at], TN)
                for b in range(part // LANE):
                    f = j // LANE + b
                    a1[e, f // NZ, f % NZ] = value[:, b * LANE : (b + 1) * LANE].astype(BF)
            clock.busy(1.5)
            clock.spawn(sum_grads(e))
            yield 0.0
            for j in range(0, width, part):
                at = pl.ds(j, part)
                for m, (left, right) in enumerate(((gat, xin), (uat, xin), (ht, gin))):
                    value = dot(left[...], right[e, :, at], NN)
                    for b in range(part // LANE):
                        d = j // LANE + b
                        dw[e, d % 2, d // 4, (d // 2) % 2, m] = value[:, b * LANE : (b + 1) * LANE].astype(BF)
                clock.busy(0.6)
                yield 0.0
            clock.spawn(scatter_grads(e))

    for e in range(experts):
        copy = pltpu.make_async_copy(w_in.at[e], w_block(e, dp), local_sem.at[e])
        copy.start()
        own_block.append(copy)
    clock.spawn(gather_row(0, yh, w_in.at[0]))
    clock.spawn(gather_other(0, 16.0))
    clock.spawn(gather_other(1, 31.0))
    clock.spawn(compute())
    clock.spawn(gather_row(1, yh, w_in.at[1]), 12.0)
    clock.spawn(share_outputs(), 60.0)
    clock.spawn(share_grads(), 60.0)
    clock.run()
    for copy in sent:
        copy.wait_send()
    assert len(sent) <= NSEM, len(sent)


def body(tokens, expert_ids, route_probs, gate_w, up_w, down_w, out_grad):
    tok, width = tokens.shape
    experts, rows, hid = gate_w.shape
    assert rows == LANE and tok == 512
    slots = tok // 2
    shard = jnp.stack([gate_w.swapaxes(1, 2), up_w.swapaxes(1, 2), down_w], axis=1)
    vmem = pl.BlockSpec(memory_space=pltpu.VMEM)
    two = experts
    scratch = [
        pltpu.VMEM((two, 3, hid, width), BF),
        pltpu.VMEM((two, 2, NX, 2, 3, hid, LANE), BF),
        pltpu.VMEM((two, NX, 2, 3, hid, LANE), BF),
        pltpu.VMEM((two, 2, 2, 3, hid // 2, LANE), BF),
        pltpu.VMEM((two, 2, 2, 3, hid, LANE), BF),
        pltpu.VMEM((two, 3, hid, LANE), BF),
        pltpu.VMEM((two, 3, hid, LANE), BF),
        pltpu.VMEM((two, NZ, 2, slots, LANE), BF),
        pltpu.VMEM((two, 2, NZ, slots, LANE), BF),
        pltpu.VMEM((two, 2, NZ // 2, 2, slots, LANE), BF),
        pltpu.VMEM((two, 2, NZ // 2, slots, LANE), BF),
        pltpu.VMEM((two, slots, LANE), BF),
        pltpu.VMEM((two, slots, LANE), BF),
        pltpu.VMEM((two, NZ, slots, LANE), BF),
        pltpu.VMEM((two, slots, LANE), BF),
        pltpu.VMEM((two, slots, LANE), BF),
        pltpu.VMEM((two, slots, tok), BF),
        pltpu.VMEM((two, slots, width), BF),
        pltpu.VMEM((two, slots, width), BF),
        pltpu.VMEM((hid, slots), F32),
        pltpu.VMEM((hid, slots), F32),
        pltpu.VMEM((hid, slots), BF),
        pltpu.VMEM((hid, slots), BF),
        pltpu.VMEM((hid, slots), BF),
        pltpu.SemaphoreType.DMA((NSEM,)),
        pltpu.SemaphoreType.DMA((NSEM,)),
        pltpu.SemaphoreType.DMA((2,)),
    ]
    mixed, token_grad, grads = pl.pallas_call(
        kernel,
        out_shape=(
            jax.ShapeDtypeStruct((tok, width), BF),
            jax.ShapeDtypeStruct((tok, width), BF),
            jax.ShapeDtypeStruct((experts, 3, hid, LANE), BF),
        ),
        in_specs=[vmem] * 5,
        out_specs=(vmem, vmem, vmem),
        scratch_shapes=scratch,
        compiler_params=pltpu.CompilerParams(
            collective_id=0, has_side_effects=True, vmem_limit_bytes=67_043_328
        ),
        name="moe_layer",
    )(shard, tokens, out_grad, expert_ids.T, route_probs.T)
    return (
        mixed,
        token_grad,
        grads[:, 0].swapaxes(1, 2),
        grads[:, 1].swapaxes(1, 2),
        grads[:, 2],
    )


def solution(mesh):
    placed = (
        P("dp", None),
        P("dp", None),
        P("dp", None),
        P(None, "dp", "fsdp"),
        P(None, "dp", "fsdp"),
        P(None, "fsdp", "dp"),
        P("dp", None),
    )
    return jax.shard_map(
        body,
        mesh=mesh,
        in_specs=placed,
        out_specs=(
            P("dp", None),
            P("dp", None),
            P(None, "dp", "fsdp"),
            P(None, "dp", "fsdp"),
            P(None, "fsdp", "dp"),
        ),
        check_vma=False,
    )
```

time: 1000 us -> 165 us (0.17)
  waiting for transfers between devices: 869 us -> 0 us
  Pallas kernels: 0 us -> 156 us
  local copies, waits for them, and re-layouts: 65.4 us -> 6.65 us
  matrix products: 39.4 us -> 0 us
  between operations: 14.3 us -> 0.64 us
  other arithmetic: 13.1 us -> 2.09 us
    unnamed x19 -> x0, waiting for transfers between devices: 429 us -> none
    all_gather x6 -> x0, waiting for transfers between devices: 287 us -> none  [the longest x2 105 us: body(): lax.all_gather(gate_w[expert], 'dp', axis=0, tiled=True)]
    pallas_call x0 -> x1, Pallas kernels: none -> 156 us  [body(): pl.pallas_call(kernel, out_shape=(jax.ShapeDtypeStruct((tok, width), BF),...]
    psum x1 -> x0, waiting for transfers between devices: 153 us -> none  [group_total(): return lax.psum(partial_value.astype(jnp.bfloat16), 'fsdp')]
    dot_general x18 -> x0, matrix products: 39.4 us -> none  [the longest x2 6.97 us: body(): lax.dot_general(slot_grad, down_full, (((1,), (1,)), ((), ())), preferred...]
    gather x10 -> x0, local copies, waits for them, and re-layouts: 31.5 us -> none  [the longest x2 9.51 us: body(): jnp.take(out_grad, slot_token, axis=0).astype(jnp.float32)]
    unnamed x54 -> x4, local copies, waits for them, and re-layouts: 28.4 us -> 4.63 us
  transfers between devices with their start and end apart: 13 -> 0, of which waited for: 13 -> 0; matrix products, arithmetic and copies ran while one was open for 11% -> 0% of each run, Pallas kernels for 0% -> 0%
where the time goes in v1:
time: 165 us
  Pallas kernels  156 us (95%)
  local copies, waits for them, and re-layouts  6.65 us (4%)
  other arithmetic  2.09 us (1%)
    pallas_call x1, Pallas kernels, body(): pl.pallas_call(kernel, out_shape=(jax.ShapeDtypeStruct((tok, width), BF),...  156 us
    unnamed x4, local copies, waits for them, and re-layouts  4.63 us

profile of v1, /device:TPU:8, one launch (start us, length us, event | category | flops | bytes accessed | tf_op | source)
XLA Modules:
  0.0 165.0 jit_solution(16906362541340089027)
XLA Ops:
  0.6 2.1 %pad_maximum_fusion.w_in = bf16[2,3,448,128]{3,2,1,0:T(8,128)(2,1)} fusion(bf16[2,1,448,128]{3,2,1,0:T(8,128)(2,1)} %bitcast.19, bf16[2,1,448,128]{3,2,1,0:T(8,128)(2,1)} %bitcast.20, bf16[2,1,448,128]{3,2,1,0:T(8,128)(2,1)} %bitcast.21), kind=kLoop, calls=%fused_computation | loop fusion | flops 688128 | bytes 1376256 | tf_op jit(solution)/shard_map/stack | solution.py:450
  2.7 155.6 %moe_layer.1 = (bf16[512,2048]{1,0:T(8,128)(2,1)}, bf16[512,2048]{1,0:T(8,128)(2,1)}, bf16[2,3,448,128]{3,2,1,0:T(8,128)(2,1)}) custom-call(bf16[2,3,448,128]{3,2,1,0:T(8,128)(2,1)} %pad_maximum_fusion.w_in, bf16[512,2048]{1,0:T(8,128)(2,1)} %tok_ref.1, bf16[512,2048]{1,0:T(8,128)(2,1)} %grad_ref.1, s32[2,512]{1,0:T(2,128)} %bitcast.22, f32[2,512]{1,0:T(2,128)} %bitcast.23), custom_call_target="tpu_custom_call" | custom-call | tf_op jit(solution)/shard_map/moe_layer/pallas_call | solution.py:482
  158.3 2.0 %slice_bitcast_fusion = (bf16[2,448,128]{2,1,0:T(8,128)(2,1)}, bf16[2,128,448]{1,2,0:T(8,128)(2,1)}, bf16[2,128,448]{1,2,0:T(8,128)(2,1)}) fusion(bf16[2,3,448,128]{3,2,1,0:T(8,128)(2,1)} %get-tuple-element.10), kind=kLoop, calls=%fused_computation.1 | loop fusion | bytes 1376256 | tf_op jit(solution)/shard_map/squeeze | solution.py:502
  160.3 0.0 copy-start
  160.3 3.3 %copy.14 = bf16[512,2048]{1,0:T(8,128)(2,1)} copy(bf16[512,2048]{1,0:T(8,128)(2,1)} %get-tuple-element.19) | data formatting | bytes 4194304
  163.6 0.0 copy-done
  163.6 1.3 copy.15
Async XLA Ops:
  160.3 3.3 %copy-start = (bf16[512,2048]{1,0:T(8,128)(2,1)S(1)}, bf16[512,2048]{1,0:T(8,128)(2,1)}, u32[]{:S(2)}) copy-start(bf16[512,2048]{1,0:T(8,128)(2,1)} %get-tuple-element.20) | copy-start | bytes 6291460

commit v2 on v1

--- a/solution.py
+++ b/solution.py
@@ -76,7 +76,7 @@
     mixed_ref, tgrad_ref, wgrad_ref,
     w_all, dw, cr, xa, xb, ys, yr,
     a0, a1, z0, z1, y0s, y0r, y1r, s0, s1,
-    pick, xin, gin, gt, ut, ht, gat, uat,
+    m_all, t_all, pick, xin, gin, gt, ut, ht, gat, uat,
     send_sem, recv_sem, local_sem,
 ):
     dp, fs = lax.axis_index("dp"), lax.axis_index("fsdp")
@@ -202,7 +202,7 @@
             [piece(0).at[yh], cr.at[e, 0, yh], xb.at[e, 0, yh], xb.at[e, 1, yh], yr.at[e]],
         )
 
-    summed = [0, 0]
+    shared = [0, 0]
 
     def sum_outputs(e):
         def piece(k):
@@ -234,7 +234,8 @@
         yield 3.0
         last.wait_recv()
         add_into(s0.at[e], [piece(0).at[yl], z0.at[e, 0, h - 1, yl], z0.at[e, 1, h - 1, yl], y0r.at[e]])
-        summed[0] += 1
+        m_all[e, :, cols(fs)] = s0[e]
+        clock.spawn(share_outputs(e))
 
     def sum_grads(e):
         def piece(k):
@@ -280,48 +281,54 @@
         go_r.wait_recv()
         go_l.wait_recv()
         add_into(s1.at[e], [piece(0), y1r.at[e, 0], z1.at[e, 0, h - 1], z1.at[e, 1, h - 1]])
-        summed[1] += 1
+        t_all[e, :, cols(fs)] = s1[e]
+        clock.spawn(share_grads(e))
 
     def place(out, sums):
-        value = dot(pick[0], sums[0], TN)
-        for e in range(1, experts):
-            value = value + dot(pick[e], sums[e], TN)
-        out[:, cols(fs)] = value.astype(out.dtype)
-
-    def share_outputs():
-        while summed[0] < experts:
-            yield 1.0
-        place(mixed_ref, s0)
-
+        for j in range(0, width, part):
+            at = pl.ds(j, part)
+            value = dot(pick[0], sums[0, :, at], TN)
+            for e in range(1, experts):
+                value = value + dot(pick[e], sums[e, :, at], TN)
+            out[:, at] = value.astype(out.dtype)
+
+    def share_outputs(e):
         def at(y, k):
-            return mixed_ref.at[:, cols(y * NZ + (z + k) % NZ)]
-
-        copy = send(at(yl, 0), at(yl, 0), ylp)
+            return m_all.at[e, :, cols(y * NZ + (z + k) % NZ)]
+
+        copy = send(s0.at[e], at(yl, 0), ylp)
+        h = NZ // 2
+        go_r, go_l = {}, {}
+        go_r[0] = send(s0.at[e], at(yl, 0), zr)
+        go_l[0] = send(s0.at[e], at(yl, 0), zl)
+        yield 2.0
+        copy.wait_recv()
+        go_r[1] = send(at(1 - yl, 0), at(1 - yl, 0), zr)
+        go_l[1] = send(at(1 - yl, 0), at(1 - yl, 0), zl)
+        top, low = pl.ds(0, slots // 2), pl.ds(slots // 2, slots // 2)
+        for k in range(1, h):
+            yield 3.0
+            for i, y in enumerate((yl, 1 - yl)):
+                rows_r, rows_l = (slice(None), slice(None)) if k < h - 1 else (top, low)
+                go_r[i].wait_recv()
+                src = at(y, NZ - k).at[rows_r]
+                go_r[i] = send(src, src, zr)
+                go_l[i].wait_recv()
+                src = at(y, k).at[rows_l]
+                go_l[i] = send(src, src, zl)
         yield 3.0
-        copy.wait_recv()
-        h = NZ // 2
-        go_r = [send(at(y, 0), at(y, 0), zr) for y in range(2)]
-        go_l = [send(at(y, 0), at(y, 0), zl) for y in range(2)]
-        for k in range(1, h):
-            yield 5.0
-            for y in range(2):
-                go_r[y].wait_recv()
-                go_r[y] = send(at(y, -k + NZ), at(y, -k + NZ), zr) if k < h - 1 or y == 0 else None
-                go_l[y].wait_recv()
-                go_l[y] = send(at(y, k), at(y, k), zl) if k < h - 1 or y == 1 else None
-        yield 4.0
-        go_r[0].wait_recv()
-        go_l[1].wait_recv()
-
-    def share_grads():
-        while summed[1] < experts:
-            yield 1.0
-        place(tgrad_ref, s1)
-        ht_ = tok // 2
-        top, low = pl.ds(0, ht_), pl.ds(ht_, ht_)
+        for i in range(2):
+            go_r[i].wait_recv()
+            go_l[i].wait_recv()
+        shared[0] += 1
+        if shared[0] == experts:
+            place(mixed_ref, m_all)
+
+    def share_grads(e):
+        top, low = pl.ds(0, slots // 2), pl.ds(slots // 2, slots // 2)
 
         def at(k, rows=slice(None)):
-            return tgrad_ref.at[rows, cols(yl * NZ + (z + k) % NZ)]
+            return t_all.at[e, rows, cols(yl * NZ + (z + k) % NZ)]
 
         across = []
 
@@ -329,10 +336,10 @@
             across.append(send(at(k, rows), at(k, rows), ylp))
 
         h = NZ // 2
-        go_r, go_l = send(at(0), at(0), zr), send(at(0), at(0), zl)
-        cross(0)
+        go_r, go_l = send(s1.at[e], at(0), zr), send(s1.at[e], at(0), zl)
+        across.append(send(s1.at[e], at(0), ylp))
         for k in range(1, h):
-            yield 3.0
+            yield 2.0
             rows_r, rows_l = (slice(None), slice(None)) if k < h - 1 else (top, low)
             go_r.wait_recv()
             go_r = send(at(NZ - k, rows_r), at(NZ - k, rows_r), zr)
@@ -340,14 +347,17 @@
             go_l.wait_recv()
             go_l = send(at(k, rows_l), at(k, rows_l), zl)
             cross(k)
-        yield 3.0
+        yield 2.0
         go_r.wait_recv()
         cross(h, top)
         go_l.wait_recv()
         cross(h, low)
-        yield 4.0
+        yield 3.0
         for copy in across:
             copy.wait_recv()
+        shared[1] += 1
+        if shared[1] == experts:
+            place(tgrad_ref, t_all)
 
     def slot_rows(e):
         hit = ids_ref[...] == e
@@ -434,8 +444,6 @@
     clock.spawn(gather_other(1, 31.0))
     clock.spawn(compute())
     clock.spawn(gather_row(1, yh, w_in.at[1]), 12.0)
-    clock.spawn(share_outputs(), 60.0)
-    clock.spawn(share_grads(), 60.0)
     clock.run()
     for copy in sent:
         copy.wait_send()
@@ -467,6 +475,8 @@
         pltpu.VMEM((two, NZ, slots, LANE), BF),
         pltpu.VMEM((two, slots, LANE), BF),
         pltpu.VMEM((two, slots, LANE), BF),
+        pltpu.VMEM((two, slots, width), BF),
+        pltpu.VMEM((two, slots, width), BF),
         pltpu.VMEM((two, slots, tok), BF),
         pltpu.VMEM((two, slots, width), BF),
         pltpu.VMEM((two, slots, width), BF),

time: 165 us -> 161 us (0.976)
  Pallas kernels: 156 us -> 152 us
    pallas_call x1, Pallas kernels: 156 us -> 152 us  [body(): pl.pallas_call(kernel, out_shape=(jax.ShapeDtypeStruct((tok, width), BF),...]
where the time goes in v2:
time: 161 us
  Pallas kernels  152 us (94%)
  local copies, waits for them, and re-layouts  6.65 us (4%)
  other arithmetic  2.09 us (1%)
    pallas_call x1, Pallas kernels, body(): pl.pallas_call(kernel, out_shape=(jax.ShapeDtypeStruct((tok, width), BF),...  152 us
    unnamed x4, local copies, waits for them, and re-layouts  4.63 us

profile of v2, /device:TPU:8, one launch (start us, length us, event | category | flops | bytes accessed | tf_op | source)
XLA Modules:
  0.0 160.9 jit_solution(2475563399803359828)
XLA Ops:
  0.6 2.1 %pad_maximum_fusion.w_in = bf16[2,3,448,128]{3,2,1,0:T(8,128)(2,1)} fusion(bf16[2,1,448,128]{3,2,1,0:T(8,128)(2,1)} %bitcast.19, bf16[2,1,448,128]{3,2,1,0:T(8,128)(2,1)} %bitcast.20, bf16[2,1,448,128]{3,2,1,0:T(8,128)(2,1)} %bitcast.21), kind=kLoop, calls=%fused_computation | loop fusion | flops 688128 | bytes 1376256 | tf_op jit(solution)/shard_map/stack | solution.py:458
  2.7 151.5 %moe_layer.1 = (bf16[512,2048]{1,0:T(8,128)(2,1)}, bf16[512,2048]{1,0:T(8,128)(2,1)}, bf16[2,3,448,128]{3,2,1,0:T(8,128)(2,1)}) custom-call(bf16[2,3,448,128]{3,2,1,0:T(8,128)(2,1)} %pad_maximum_fusion.w_in, bf16[512,2048]{1,0:T(8,128)(2,1)} %tok_ref.1, bf16[512,2048]{1,0:T(8,128)(2,1)} %grad_ref.1, s32[2,512]{1,0:T(2,128)} %bitcast.22, f32[2,512]{1,0:T(2,128)} %bitcast.23), custom_call_target="tpu_custom_call" | custom-call | tf_op jit(solution)/shard_map/moe_layer/pallas_call | solution.py:492
  154.2 2.0 %slice_bitcast_fusion = (bf16[2,448,128]{2,1,0:T(8,128)(2,1)}, bf16[2,128,448]{1,2,0:T(8,128)(2,1)}, bf16[2,128,448]{1,2,0:T(8,128)(2,1)}) fusion(bf16[2,3,448,128]{3,2,1,0:T(8,128)(2,1)} %get-tuple-element.10), kind=kLoop, calls=%fused_computation.1 | loop fusion | bytes 1376256 | tf_op jit(solution)/shard_map/squeeze | solution.py:512
  156.3 0.0 copy-start
  156.3 3.3 %copy.14 = bf16[512,2048]{1,0:T(8,128)(2,1)} copy(bf16[512,2048]{1,0:T(8,128)(2,1)} %get-tuple-element.19) | data formatting | bytes 4194304
  159.6 0.0 copy-done
  159.6 1.3 copy.15
Async XLA Ops:
  156.3 3.3 %copy-start = (bf16[512,2048]{1,0:T(8,128)(2,1)S(1)}, bf16[512,2048]{1,0:T(8,128)(2,1)}, u32[]{:S(2)}) copy-start(bf16[512,2048]{1,0:T(8,128)(2,1)} %get-tuple-element.20) | copy-start | bytes 6291460

commit v3 on v2

--- a/solution.py
+++ b/solution.py
@@ -177,7 +177,7 @@
         yield 1.0
         copies[3].wait_recv()
         add_into(piece(3), [piece(3), cr.at[e, 3]])
-        yield 6.0
+        yield 4.0
         go_r.wait_recv()
         at = dw.at[e, c, (x + 1) % NX, :, :, top]
         add_into(at, [at, xa.at[e, 0]], 32)
@@ -189,7 +189,7 @@
         on_l = send(piece(3), xb.at[e, 1], xl)
         yield 1.0
         copies[0].wait_recv()
-        yield 14.0
+        yield 10.0
         on_r.wait_recv()
         on_l.wait_recv()
         other = 1 - yh

time: 161 us -> 161 us (level)
  no operation moved by 1% of the time
where the time goes in v3:
time: 161 us
  Pallas kernels  152 us (94%)
  local copies, waits for them, and re-layouts  6.65 us (4%)
  other arithmetic  2.09 us (1%)
    pallas_call x1, Pallas kernels, body(): pl.pallas_call(kernel, out_shape=(jax.ShapeDtypeStruct((tok, width), BF),...  152 us
    unnamed x4, local copies, waits for them, and re-layouts  4.63 us

profile of v3, /device:TPU:8, one launch (start us, length us, event | category | flops | bytes accessed | tf_op | source)
XLA Modules:
  0.0 161.1 jit_solution(7807043850850539741)
XLA Ops:
  0.6 2.1 %pad_maximum_fusion.w_in = bf16[2,3,448,128]{3,2,1,0:T(8,128)(2,1)} fusion(bf16[2,1,448,128]{3,2,1,0:T(8,128)(2,1)} %bitcast.19, bf16[2,1,448,128]{3,2,1,0:T(8,128)(2,1)} %bitcast.20, bf16[2,1,448,128]{3,2,1,0:T(8,128)(2,1)} %bitcast.21), kind=kLoop, calls=%fused_computation | loop fusion | flops 688128 | bytes 1376256 | tf_op jit(solution)/shard_map/stack | solution.py:458
  2.7 151.8 %moe_layer.1 = (bf16[512,2048]{1,0:T(8,128)(2,1)}, bf16[512,2048]{1,0:T(8,128)(2,1)}, bf16[2,3,448,128]{3,2,1,0:T(8,128)(2,1)}) custom-call(bf16[2,3,448,128]{3,2,1,0:T(8,128)(2,1)} %pad_maximum_fusion.w_in, bf16[512,2048]{1,0:T(8,128)(2,1)} %tok_ref.1, bf16[512,2048]{1,0:T(8,128)(2,1)} %grad_ref.1, s32[2,512]{1,0:T(2,128)} %bitcast.22, f32[2,512]{1,0:T(2,128)} %bitcast.23), custom_call_target="tpu_custom_call" | custom-call | tf_op jit(solution)/shard_map/moe_layer/pallas_call | solution.py:492
  154.5 2.0 %slice_bitcast_fusion = (bf16[2,448,128]{2,1,0:T(8,128)(2,1)}, bf16[2,128,448]{1,2,0:T(8,128)(2,1)}, bf16[2,128,448]{1,2,0:T(8,128)(2,1)}) fusion(bf16[2,3,448,128]{3,2,1,0:T(8,128)(2,1)} %get-tuple-element.10), kind=kLoop, calls=%fused_computation.1 | loop fusion | bytes 1376256 | tf_op jit(solution)/shard_map/squeeze | solution.py:512
  156.5 0.0 copy-start
  156.5 3.3 %copy.14 = bf16[512,2048]{1,0:T(8,128)(2,1)} copy(bf16[512,2048]{1,0:T(8,128)(2,1)} %get-tuple-element.19) | data formatting | bytes 4194304
  159.8 0.0 copy-done
  159.8 1.3 copy.15
Async XLA Ops:
  156.5 3.3 %copy-start = (bf16[512,2048]{1,0:T(8,128)(2,1)S(1)}, bf16[512,2048]{1,0:T(8,128)(2,1)}, u32[]{:S(2)}) copy-start(bf16[512,2048]{1,0:T(8,128)(2,1)} %get-tuple-element.20) | copy-start | bytes 6291460
